TPU v7x, 128 devices: a whole 4x4x4 slice. The times are simulated.
128 devices in a mesh: obs: 4 (over z_hi, core), par: 32 (over y, x, z_lo).
Axes of the slice: x: 4, y: 4, z: 4 (z_hi: 2, z_lo: 2; z = z_hi * 2 + z_lo), core: 2. Of those that a mesh axis runs over, the one named last changes fastest.
Arguments:
- jacobian: bfloat16 [3072, 16384], P(('obs', 'par')), may hold values from -0.109375 to 0.109375
- obs_weights: float32 [3072], replicated, may hold values from 0.1 to 10
- time_to_obs: int32 [3072], P(('obs', 'par')), may hold values from 0 to 3071, each once
Outputs:
- normal_matrix: float32 [16384, 16384], P('obs', 'par')
Inputs may be any that keep to these rules, and one draw needn't show every extreme that they name: `time_to_obs`: each observation index appears exactly once.
All inputs are finite; a program needn't handle non-finite values.
Results may differ from a plain program's by a relative error of at most 0.0039.
Values may be sent and summed in bfloat16 or wider, within the bound.
No kernel may reach another device: no remote copies, remote signals or barrier semaphores. Data moves between devices by JAX's collectives and lax.ppermute only.
A program may use at most 128 MiB of HBM per device.

v0:
```python
import jax
import jax.numpy as jnp
from jax import lax
from jax.sharding import PartitionSpec as P


def on_device(jacobian, obs_weights, time_to_obs):
    rows_here = jacobian.shape[0]
    param_count = jacobian.shape[1]
    obs_count = lax.axis_size("obs")
    par_count = lax.axis_size("par")
    indices = jnp.arange(obs_weights.shape[0], dtype=jnp.int32)
    picked = jnp.sum(
        jnp.where(time_to_obs[:, None] == indices[None, :], obs_weights[None, :], 0.0), axis=1
    )
    scaled = (jnp.sqrt(picked)[:, None] * jacobian.astype(jnp.float32)).astype(jnp.bfloat16)
    lifted = scaled.reshape(1, rows_here, param_count)
    blocks = lax.all_to_all(lifted, "obs", split_axis=2, concat_axis=0, tiled=True)
    col_width = param_count // par_count
    columns = lax.all_to_all(lifted, "par", split_axis=2, concat_axis=0, tiled=True)
    columns = lax.all_gather(columns, "obs", axis=0, tiled=True)
    columns = columns.reshape(obs_count, par_count * rows_here, col_width)
    panels = lax.all_gather(blocks, "par", axis=1, tiled=True)
    return jnp.einsum("arc,ard->cd", panels, columns, preferred_element_type=jnp.float32)


def solution(mesh):
    placed = (P(("obs", "par"), None), P(), P(("obs", "par")))
    return jax.shard_map(
        on_device, mesh=mesh, in_specs=placed, out_specs=P("obs", "par"), check_vma=False
    )
```

profile of v0, /device:TPU:34, one launch (start us, length us, event | category | flops | bytes accessed | tf_op | source)
XLA Modules:
  0.0 776.7 jit_solution(6125067894253872118)
XLA Ops:
  6.5 0.9 select_reduce_fusion
  7.5 1.3 fusion.5
  8.8 12.5 %copy.17 = bf16[1,24,16384]{1,0,2:T(2,128)(2,1)} copy(bf16[1,24,16384]{2,1,0:T(8,128)(2,1)S(1)} %fusion.5) | data formatting | bytes 1572864 | tf_op jit(solution)/shard_map/reshape | solution.py:17
  21.3 0.5 broadcast.2
  21.8 90.6 %reduce.1 = bf16[16384,24]{1,0:T(8,128)(2,1)} reduce(bf16[16384,1,24]{2,1,0:T(2,128)(2,1)} %bitcast.26, bf16[]{:T(256)} %broadcast.2), dimensions={1}, to_apply=%bitcast.22.reduce_sub_computation | reduce | bytes 1572866
  112.5 6.6 reshape.19
  119.1 17.2 %all_to_all.36 = bf16[4,2,49152]{2,1,0:T(2,128)(2,1)S(1)} all-to-all(bf16[4,2,49152]{2,1,0:T(2,128)(2,1)S(1)} %reshape.19), channel_id=1, replica_groups=mesh['obs'=4,'par'=32] {'obs'}, dimensions={0} | all-to-all | bytes 1572864 | tf_op jit(solution)/shard_map/all_to_all | solution.py:18
  136.3 12.0 %reshape.20 = bf16[16384,1,24]{2,1,0:T(2,128)(2,1)} reshape(bf16[4,2,49152]{2,1,0:T(2,128)(2,1)S(1)} %all_to_all.36) | data formatting | bytes 1572864
  148.3 15.2 %copy.18 = bf16[1,24,16384]{2,1,0:T(8,128)(2,1)S(1)} copy(bf16[1,24,16384]{1,0,2:T(2,128)(2,1)} %bitcast.28) | data formatting | bytes 1572864 | tf_op jit(solution)/shard_map/all_to_all | solution.py:18
  163.5 1.5 all_to_all.27
  165.0 0.0 all-gather.5.cloned.1.call-update
  165.0 0.2 all-gather.7.cloned.1.call-start
  165.2 90.7 %reduce = bf16[16384,24]{1,0:T(8,128)(2,1)} reduce(bf16[16384,1,24]{2,1,0:T(2,128)(2,1)} %bitcast.27, bf16[]{:T(256)} %broadcast.2), dimensions={1}, to_apply=%bitcast.20.reduce_sub_computation | reduce | bytes 1572866
  255.9 7.4 reshape.17
  263.3 23.5 %all_to_all.37 = bf16[32,2,6144]{2,1,0:T(2,128)(2,1)S(1)} all-to-all(bf16[32,2,6144]{2,1,0:T(2,128)(2,1)S(1)} %reshape.17), channel_id=1, replica_groups=mesh['obs'=4,'par'=32] {'par'}, dimensions={0} | all-to-all | bytes 1572864 | tf_op jit(solution)/shard_map/all_to_all | solution.py:20
  286.8 17.3 %reshape.18 = bf16[16384,1,24]{2,1,0:T(2,128)(2,1)} reshape(bf16[32,2,6144]{2,1,0:T(2,128)(2,1)S(1)} %all_to_all.37) | data formatting | bytes 1572864
  304.1 15.2 %copy.22 = bf16[1,24,16384]{2,1,0:T(8,128)(2,1)S(1)} copy(bf16[1,24,16384]{1,0,2:T(2,128)(2,1)} %bitcast.29) | data formatting | bytes 1572864 | tf_op jit(solution)/shard_map/all_to_all | solution.py:20
  319.3 0.2 copy.24
  319.6 0.1 bitcast_bitcast_fusion
  319.6 1.3 copy.23
  320.9 0.0 all-gather.7.cloned.1.call-update
  321.0 388.9 %all-gather.5.cloned.1.call-done = bf16[4,1,768,4096]{3,0,1,2:T(4,128)(2,1)} async-done(((bf16[4,1,24,4096]{3,0,1,2:T(4,128)(2,1)}), bf16[4,1,768,4096]{3,0,1,2:T(4,128)(2,1)}) %all-gather.5.cloned.1.call-update) | async-done | bytes 25165840 | tf_op jit(solution)/shard_map/all_gather | solution.py:23
  709.9 39.0 %copy.20 = bf16[4,1,768,4096]{2,3,0,1:T(8,128)(2,1)} copy(bf16[4,1,768,4096]{3,0,1,2:T(4,128)(2,1)} %all-gather.5.cloned.1.call-done) | data formatting | bytes 50331648 | tf_op jit(solution)/shard_map/all_gather | solution.py:23
  748.9 20.9 %fusion.2 = f32[4096,512]{1,0:T(8,128)} fusion(bf16[4,768,512]{2,1,0:T(8,128)(2,1)} %bitcast.33, bf16[4,1,768,4096]{2,3,0,1:T(8,128)(2,1)} %copy.20), kind=kOutput, calls=%fused_computation.2 | convolution fusion | flops 12884901888 | bytes 36700160 | tf_op jit(solution)/shard_map/arc,ard->cd/dot_general | solution.py:24
  (3 shorter events, 0.0 us)
Async XLA Ops:
  6.5 703.4 %all-gather.5.cloned.1.call-start = ((), (), s32[]{:S(2)}) async-start(), calls=%async_computation.2 | async-start | bytes 25952256 | tf_op jit(solution)/shard_map/all_gather | solution.py:23
  165.0 583.9 %all-gather.7.cloned.1.call-start = ((), (), s32[]{:S(2)}) async-start(), calls=%async_computation.3 | async-start | bytes 3932160 | tf_op jit(solution)/shard_map/all_gather | solution.py:21
Sparse Core Ops, SparseCore 0:
  165.1 544.7 all-gather.4
  711.6 31.3 all-gather.6
where the time goes:
time: 779 us; the launch traced here: 777 us
  waiting for transfers between devices  389 us (50%)
  other arithmetic  184 us (24%)
  local copies, waits for them, and re-layouts  129 us (17%)
  blocking collectives  40.7 us (5%)
  matrix products  20.9 us (3%)
  between operations  13.5 us (2%)
    all_gather x1, waiting for transfers between devices, on_device(): panels = lax.all_gather(blocks, 'par', axis=1, tiled=True)  389 us
    unnamed x2, other arithmetic  181 us
    unnamed x6, local copies, waits for them, and re-layouts  44.1 us
    all_gather x1, local copies, waits for them, and re-layouts, on_device(): panels = lax.all_gather(blocks, 'par', axis=1, tiled=True)  39 us
    all_to_all x1, blocking collectives, on_device(): lax.all_to_all(lifted, 'par', split_axis=2, concat_axis=0, tiled=True)  23.5 us
    dot_general x1, matrix products, on_device(): jnp.einsum('arc,ard->cd', panels, columns, preferred_element_type=jnp.flo...  20.9 us
    all_to_all x1, blocking collectives, on_device(): lax.all_to_all(lifted, 'obs', split_axis=2, concat_axis=0, tiled=True)  17.2 us
    all_to_all x2, local copies, waits for them, and re-layouts, on_device(): lax.all_to_all(lifted, 'obs', split_axis=2, concat_axis=0, tiled=True)  16.7 us
  transfers between devices with their start and end apart: 2, of which 1 were waited for; matrix products, arithmetic and copies ran while one was open for 22% of the time, Pallas kernels for 0%

commit v1 on v0

--- a/solution.py
+++ b/solution.py
@@ -5,6 +5,20 @@
 
 
 def on_device(jacobian, obs_weights, time_to_obs):
+
+    def step_on_links(named_axis, in_array, which_dim, on_dim):
+        return jnp.concatenate(
+            lax.all_to_all(
+                jnp.stack(
+                    jnp.split(in_array, lax.psum(1, axis_name=named_axis), axis=which_dim), axis=0
+                ),
+                axis_name=named_axis,
+                split_axis=0,
+                concat_axis=0,
+            ),
+            axis=on_dim,
+        )
+
     rows_here = jacobian.shape[0]
     param_count = jacobian.shape[1]
     obs_count = lax.axis_size("obs")
@@ -15,7 +29,7 @@
     )
     scaled = (jnp.sqrt(picked)[:, None] * jacobian.astype(jnp.float32)).astype(jnp.bfloat16)
     lifted = scaled.reshape(1, rows_here, param_count)
-    blocks = lax.all_to_all(lifted, "obs", split_axis=2, concat_axis=0, tiled=True)
+    blocks = step_on_links("obs", in_array=lifted, which_dim=2, on_dim=0)
     col_width = param_count // par_count
     columns = lax.all_to_all(lifted, "par", split_axis=2, concat_axis=0, tiled=True)
     columns = lax.all_gather(columns, "obs", axis=0, tiled=True)

time: 779 us -> 641 us (0.82)
  other arithmetic: 184 us -> 93.1 us
  local copies, waits for them, and re-layouts: 129 us -> 95.1 us
  waiting for transfers between devices: 389 us -> 376 us
    unnamed x2 -> x1, other arithmetic: 181 us -> 90.7 us
    unnamed x6 -> x4, local copies, waits for them, and re-layouts: 44.1 us -> 25.5 us
    all_to_all x2 -> x1, local copies, waits for them, and re-layouts: 16.7 us -> 1.53 us  [step_on_links(): lax.all_to_all(jnp.stack(jnp.split(in_array, lax.psum(1, axis_name=named_...]
    all_gather x1, waiting for transfers between devices: 389 us -> 376 us  [on_device(): panels = lax.all_gather(blocks, 'par', axis=1, tiled=True)]
  transfers between devices with their start and end apart: 2 -> 2, of which waited for: 1 -> 1; matrix products, arithmetic and copies ran while one was open for 22% -> 29% of each run, Pallas kernels for 0% -> 0%
where the time goes in v1:
time: 641 us; the launch traced here: 639 us
  waiting for transfers between devices  376 us (59%)
  local copies, waits for them, and re-layouts  95.1 us (15%)
  other arithmetic  93.1 us (15%)
  blocking collectives  41 us (6%)
  matrix products  20.9 us (3%)
  between operations  13.5 us (2%)
    all_gather x1, waiting for transfers between devices, on_device(): panels = lax.all_gather(blocks, 'par', axis=1, tiled=True)  376 us
    unnamed x1, other arithmetic  90.7 us
    all_gather x1, local copies, waits for them, and re-layouts, on_device(): panels = lax.all_gather(blocks, 'par', axis=1, tiled=True)  38.9 us
    unnamed x4, local copies, waits for them, and re-layouts  25.5 us
    all_to_all x1, blocking collectives, on_device(): lax.all_to_all(lifted, 'par', split_axis=2, concat_axis=0, tiled=True)  23.8 us
    dot_general x1, matrix products, on_device(): jnp.einsum('arc,ard->cd', panels, columns, preferred_element_type=jnp.flo...  20.9 us
    all_to_all x1, blocking collectives, step_on_links(): lax.all_to_all(jnp.stack(jnp.split(in_array, lax.psum(1, axis_name=named_...  17.2 us
    all_to_all x3, local copies, waits for them, and re-layouts, on_device(): lax.all_to_all(lifted, 'par', split_axis=2, concat_axis=0, tiled=True)  16.6 us
  transfers between devices with their start and end apart: 2, of which 1 were waited for; matrix products, arithmetic and copies ran while one was open for 29% of the time, Pallas kernels for 0%

profile of v1, /device:TPU:34, one launch (start us, length us, event | category | flops | bytes accessed | tf_op | source)
XLA Modules:
  0.0 639.3 jit_solution(7465687384219261055)
XLA Ops:
  6.5 0.0 all-gather.5.cloned.1.call-start
  6.5 0.9 select_reduce_fusion
  7.5 1.3 fusion.5
  8.8 0.1 slice_bitcast_fusion.3
  8.9 0.1 pad_maximum_fusion
  9.0 17.2 %all_to_all.23 = bf16[4,1,24,4096]{3,2,1,0:T(8,128)(2,1)S(1)} all-to-all(bf16[4,1,24,4096]{3,2,1,0:T(8,128)(2,1)S(1)} %pad_maximum_fusion), channel_id=1, replica_groups=mesh['obs'=4,'par'=32] {'obs'}, dimensions={0} | all-to-all | bytes 1572864 | tf_op jit(solution)/shard_map/all_to_all | solution.py:11
  26.2 1.5 copy.22
  27.7 0.0 all-gather.5.cloned.1.call-update
  27.7 0.0 all-gather.7.cloned.1.call-start
  27.8 12.5 %copy.24 = bf16[1,24,16384]{1,0,2:T(2,128)(2,1)} copy(bf16[1,24,16384]{2,1,0:T(8,128)(2,1)S(1)} %fusion.5) | data formatting | bytes 1572864 | tf_op jit(solution)/shard_map/reshape | solution.py:31
  40.3 0.6 broadcast.2
  40.9 90.7 %reduce = bf16[16384,24]{1,0:T(8,128)(2,1)} reduce(bf16[16384,1,24]{2,1,0:T(2,128)(2,1)} %bitcast.29, bf16[]{:T(256)} %broadcast.2), dimensions={1}, to_apply=%bitcast.25.reduce_sub_computation | reduce | bytes 1572866
  131.6 7.4 %reshape.21 = bf16[32,2,6144]{2,1,0:T(2,128)(2,1)S(1)} reshape(bf16[16384,24]{1,0:T(8,128)(2,1)} %reduce) | data formatting | bytes 1572864
  139.0 23.8 %all_to_all.24 = bf16[32,2,6144]{2,1,0:T(2,128)(2,1)S(1)} all-to-all(bf16[32,2,6144]{2,1,0:T(2,128)(2,1)S(1)} %reshape.21), channel_id=1, replica_groups=mesh['obs'=4,'par'=32] {'par'}, dimensions={0} | all-to-all | bytes 1572864 | tf_op jit(solution)/shard_map/all_to_all | solution.py:34
  162.8 17.3 %reshape.22 = bf16[16384,1,24]{2,1,0:T(2,128)(2,1)} reshape(bf16[32,2,6144]{2,1,0:T(2,128)(2,1)S(1)} %all_to_all.24) | data formatting | bytes 1572864
  180.2 15.2 %copy.25 = bf16[1,24,16384]{2,1,0:T(8,128)(2,1)S(1)} copy(bf16[1,24,16384]{1,0,2:T(2,128)(2,1)} %bitcast.30) | data formatting | bytes 1572864 | tf_op jit(solution)/shard_map/all_to_all | solution.py:34
  195.4 0.2 copy.27
  195.6 0.1 bitcast_bitcast_fusion
  195.7 1.3 copy.26
  197.0 0.0 all-gather.7.cloned.1.call-update
  197.0 375.6 %all-gather.5.cloned.1.call-done = bf16[4,1,768,4096]{3,0,1,2:T(4,128)(2,1)} async-done(((bf16[4,1,24,4096]{3,0,1,2:T(4,128)(2,1)}), bf16[4,1,768,4096]{3,0,1,2:T(4,128)(2,1)}) %all-gather.5.cloned.1.call-update) | async-done | bytes 25165840 | tf_op jit(solution)/shard_map/all_gather | solution.py:37
  572.7 38.9 %copy.23 = bf16[4,1,768,4096]{2,3,0,1:T(8,128)(2,1)} copy(bf16[4,1,768,4096]{3,0,1,2:T(4,128)(2,1)} %all-gather.5.cloned.1.call-done) | data formatting | bytes 50331648 | tf_op jit(solution)/shard_map/all_gather | solution.py:37
  611.6 0.0 all-gather.7.cloned.1.call-done
  611.6 20.9 %fusion.2 = f32[4096,512]{1,0:T(8,128)} fusion(bf16[4,768,512]{2,1,0:T(8,128)(2,1)} %bitcast.33, bf16[4,1,768,4096]{2,3,0,1:T(8,128)(2,1)} %copy.23), kind=kOutput, calls=%fused_computation.2 | convolution fusion | flops 12884901888 | bytes 36700160 | tf_op jit(solution)/shard_map/arc,ard->cd/dot_general | solution.py:38
  (1 shorter events, 0.0 us)
Async XLA Ops:
  6.5 566.1 %all-gather.5.cloned.1.call-start = ((), (), s32[]{:S(2)}) async-start(), calls=%async_computation.2 | async-start | bytes 25952256 | tf_op jit(solution)/shard_map/all_gather | solution.py:37
  27.7 583.9 %all-gather.7.cloned.1.call-start = ((), (), s32[]{:S(2)}) async-start(), calls=%async_computation.3 | async-start | bytes 3932160 | tf_op jit(solution)/shard_map/all_gather | solution.py:35
Sparse Core Ops, SparseCore 0:
  27.9 544.7 all-gather.4
  574.3 31.3 all-gather.6
